TPU v7x, 256 devices: a whole 4x4x8 slice. The times are simulated.
256 devices in a mesh: dp: 8 (over x, core), ctx: 32 (over y, z).
Axes of the slice: x: 4, y: 4, z: 8, core: 2. Of those that a mesh axis runs over, the one named last changes fastest.
Arguments:
- features: bfloat16 [8, 4096, 6144], P('dp', 'ctx'), may hold values from -6 to 6
- upstream: bfloat16 [8, 4096, 2048], P('dp', 'ctx'), may hold values from -6 to 6
- lengths: int32 [8, 8], P('dp'), may hold values from 1 to 2048, 4096 in all within a row
- conv_taps: float32 [3, 6144], replicated, may hold values from -3 to 3
- residues: float32 [16, 2048], P(None, 'ctx'), may hold values from -0.12 to 0.12
- log_rate: float32 [16, 2048], P(None, 'ctx'), may hold values from -13.2 to -3.5
- skip_gain: float32 [2048], P('ctx'), may hold values from -4 to 4
Outputs:
- grad_features: bfloat16 [8, 4096, 6144], P('dp', 'ctx')
- grad_taps: float32 [3, 6144], replicated
- grad_residues: float32 [16, 2048], P(None, 'ctx')
- grad_skip: float32 [2048], P('ctx')
All inputs are finite; a program needn't handle non-finite values.
Results may differ from a plain program's by a relative error of at most 0.0095.
Values may be sent and summed in bfloat16 or wider, within the bound.
A program may use at most 192 MiB of HBM per device.

v0:
```python
import math
import jax
import jax.numpy as jnp
from jax import lax
from jax.sharding import PartitionSpec as P

BLOCK_ROWS = 128


def from_behind(block, axis, distance):
    devices = range(lax.axis_size(axis))
    route = [(i - distance, i) for i in devices if i - distance in devices]
    return lax.ppermute(block, axis, route)


def segment_of(positions, bounds):
    return jnp.sum((positions[:, None] >= bounds[None, :]).astype(jnp.int32), axis=1)


def segment_masks(positions, bounds, window_len):
    seg_ids = segment_of(positions, bounds)
    keep_one = ((positions >= 1) & (segment_of(positions - 1, bounds) == seg_ids)).astype(
        jnp.float32
    )
    keep_two = ((positions >= 2) & (segment_of(positions - 2, bounds) == seg_ids)).astype(
        jnp.float32
    )
    next_one = (
        (positions + 1 < window_len) & (segment_of(positions + 1, bounds) == seg_ids)
    ).astype(jnp.float32)
    next_two = (
        (positions + 2 < window_len) & (segment_of(positions + 2, bounds) == seg_ids)
    ).astype(jnp.float32)
    return (seg_ids, keep_one, keep_two, next_one, next_two)


def causal_taps(current, before, tap_rows, keep_one, keep_two):
    extended = jnp.concatenate([before, current], axis=0)
    return (
        tap_rows[0] * current
        + tap_rows[1] * (keep_one[:, None] * extended[1:-1])
        + tap_rows[2] * (keep_two[:, None] * extended[:-2])
    )


def transposed_taps(current, after, tap_rows, next_one, next_two):
    extended = jnp.concatenate([current, after], axis=0)
    return (
        tap_rows[0] * current
        + tap_rows[1] * (next_one[:, None] * extended[1:-1])
        + tap_rows[2] * (next_two[:, None] * extended[2:])
    )


def tap_terms(gradient, current, before, keep_one, keep_two):
    extended = jnp.concatenate([before, current], axis=0)
    first = jnp.sum(gradient * current, axis=0)
    second = jnp.sum(gradient * (keep_one[:, None] * extended[1:-1]), axis=0)
    third = jnp.sum(gradient * (keep_two[:, None] * extended[:-2]), axis=0)
    return jnp.stack([first, second, third])


def combine_states(earlier, later):
    return (earlier[0] * later[0], later[0] * earlier[1] + later[1])


def modal_sweep(source, segment_ids, decay_rate, coeff, other):
    length, chan_count = source.shape
    pole_count = decay_rate.shape[0]
    blocks = length // BLOCK_ROWS
    per_step = 4
    groups = blocks // per_step
    offsets = jnp.arange(BLOCK_ROWS, dtype=jnp.float32)
    rising = jnp.exp(decay_rate[None] * offsets[:, None, None])
    falling = jnp.exp(-decay_rate[None] * offsets[:, None, None])
    causal = offsets[:, None] >= offsets[None, :]

    def group_fn(inputs):
        src_blk, seg_blk, other_blk = inputs
        joined_mask = ((seg_blk[:, :, None] == seg_blk[:, None, :]) & causal[None]).astype(
            source.dtype
        )
        lifted = (src_blk[:, :, None, :] * rising[None]).reshape(
            per_step, BLOCK_ROWS, pole_count * chan_count
        )
        inner_state = jnp.einsum(
            "pij,pjk->pik", joined_mask, lifted, precision=lax.Precision.HIGHEST
        )
        inner_state = (
            inner_state.reshape(per_step, BLOCK_ROWS, pole_count, chan_count) * falling[None]
        )
        block_out = jnp.einsum("pimc,mc->pic", inner_state, coeff, precision=lax.Precision.HIGHEST)
        last_row = inner_state[:, -1]
        start_same = (seg_blk == seg_blk[:, :1]).astype(source.dtype)
        partial_sum = jnp.einsum(
            "pic,pimc->mc", other_blk, inner_state, precision=lax.Precision.HIGHEST
        )
        weights = jnp.einsum(
            "pic,imc->pmc",
            other_blk * start_same[:, :, None],
            falling,
            precision=lax.Precision.HIGHEST,
        )
        return (block_out, last_row, partial_sum, weights)

    src_groups = source.reshape(groups, per_step, BLOCK_ROWS, chan_count)
    seg_groups = segment_ids.reshape(groups, per_step, BLOCK_ROWS)
    other_groups = other.reshape(groups, per_step, BLOCK_ROWS, chan_count)
    block_out, last_row, partial_sum, weights = lax.map(
        group_fn, (src_groups, seg_groups, other_groups)
    )
    block_out = block_out.reshape(blocks, BLOCK_ROWS, chan_count)
    last_row = last_row.reshape(blocks, pole_count, chan_count)
    weights = weights.reshape(blocks, pole_count, chan_count)
    seg_rows = segment_ids.reshape(blocks, BLOCK_ROWS)
    starts = seg_rows[:, 0]
    finals = seg_rows[:, -1]
    joined = (starts[1:] == finals[:-1]).astype(source.dtype)
    through = (starts[:-1] == finals[:-1]).astype(source.dtype)
    one_step = jnp.exp(-decay_rate)
    block_decay = jnp.exp(-decay_rate * BLOCK_ROWS)
    factors = (joined * through)[:, None, None] * block_decay[None]
    inputs_in = joined[:, None, None] * one_step[None] * last_row[:-1]
    unused, states = lax.associative_scan(combine_states, (factors, inputs_in))
    carried = jnp.concatenate(
        [jnp.zeros((1, pole_count, chan_count), source.dtype), states], axis=0
    )
    start_rows = (seg_rows == starts[:, None]).astype(source.dtype)
    carry_out = (
        jnp.einsum("kmc,imc->kic", carried * coeff[None], falling, precision=lax.Precision.HIGHEST)
        * start_rows[:, :, None]
    )
    result = (block_out + carry_out).reshape(length, chan_count)
    grad_part = jnp.sum(partial_sum, axis=0) + jnp.einsum(
        "kmc,kmc->mc", weights, carried, precision=lax.Precision.HIGHEST
    )
    return (result, grad_part)


def per_device(features, upstream, lengths, conv_taps, residues, log_rate, skip_gain):
    feats = features[0]
    upf = upstream[0].astype(jnp.float32)
    tok_rows = feats.shape[0]
    channels = upstream.shape[2]
    ctx_count = lax.axis_size("ctx")
    shard_index = lax.axis_index("ctx")
    per_shard = channels // ctx_count
    window_len = tok_rows * ctx_count
    grad_scale = 1.0 / math.sqrt(window_len * lax.axis_size("dp"))
    bounds = jnp.cumsum(lengths[0])[:-1]
    local_pos = shard_index * tok_rows + jnp.arange(tok_rows, dtype=jnp.int32)
    seg_local, keep_one, keep_two, next_one, next_two = segment_masks(local_pos, bounds, window_len)
    whole_pos = jnp.arange(window_len, dtype=jnp.int32)
    seg_all, wkeep_one, wkeep_two, wnext_one, wnext_two = segment_masks(
        whole_pos, bounds, window_len
    )
    decay_rate = jnp.exp(log_rate)
    zero_rows = jnp.zeros((2, per_shard), jnp.float32)
    edge_rows = feats[-2:, :channels]
    before = from_behind(edge_rows, "ctx", 1).astype(jnp.float32)
    src_seq = feats[:, :channels].astype(jnp.float32)
    query_seq = causal_taps(src_seq, before, conv_taps[:, :channels], keep_one, keep_two)
    outgoing = feats[:, channels:].reshape(tok_rows, 2, channels)
    grad_out = (upf * query_seq).astype(jnp.bfloat16)[:, None, :]
    arrived = lax.all_to_all(outgoing, "ctx", split_axis=2, concat_axis=0, tiled=True)
    arrived_grad = lax.all_to_all(grad_out, "ctx", split_axis=2, concat_axis=0, tiled=True)
    tap_cols = lax.dynamic_slice(
        conv_taps.reshape(3, 3, channels), (0, 1, shard_index * per_shard), (3, 2, per_shard)
    )
    key_src = arrived[:, 0].astype(jnp.float32)
    val_src = arrived[:, 1].astype(jnp.float32)
    key_ch = causal_taps(key_src, zero_rows, tap_cols[:, 0], wkeep_one, wkeep_two)
    val_ch = causal_taps(val_src, zero_rows, tap_cols[:, 1], wkeep_one, wkeep_two)
    mixed_ch = (key_ch * val_ch).astype(jnp.bfloat16)
    mixedf = mixed_ch.astype(jnp.float32)
    conv_out, unused = modal_sweep(mixedf, seg_all, decay_rate, residues, jnp.zeros_like(mixedf))
    output_ch = (conv_out + skip_gain * mixedf).astype(jnp.bfloat16)
    gradf = arrived_grad[:, 0].astype(jnp.float32)
    adjoint, grad_resid = modal_sweep(
        gradf[::-1], seg_all[::-1], decay_rate, residues, mixedf[::-1]
    )
    grad_mixed = (adjoint[::-1] + skip_gain * gradf).astype(jnp.bfloat16)
    skip_part = jnp.sum(mixedf * gradf, axis=0)
    dmixf = grad_mixed.astype(jnp.float32)
    grad_key = dmixf * val_ch
    grad_val = dmixf * key_ch
    key_back = transposed_taps(grad_key, zero_rows, tap_cols[:, 0], wnext_one, wnext_two)
    val_back = transposed_taps(grad_val, zero_rows, tap_cols[:, 1], wnext_one, wnext_two)
    second = jnp.stack([key_back, val_back], axis=1).astype(jnp.bfloat16)
    kv_taps = jnp.stack(
        [
            tap_terms(grad_key, key_src, zero_rows, wkeep_one, wkeep_two),
            tap_terms(grad_val, val_src, zero_rows, wkeep_one, wkeep_two),
        ],
        axis=1,
    )
    first = output_ch[:, None, :]
    first_back = lax.all_to_all(first, "ctx", split_axis=0, concat_axis=2, tiled=True)
    second_back = lax.all_to_all(second, "ctx", split_axis=0, concat_axis=2, tiled=True)
    grad_query = upf * first_back[:, 0].astype(jnp.float32)
    rows_next = from_behind(grad_query[:2], "ctx", -1)
    grad_query_feats = transposed_taps(
        grad_query, rows_next, conv_taps[:, :channels], next_one, next_two
    ).astype(jnp.bfloat16)
    grad_feats = jnp.concatenate(
        [grad_query_feats, second_back.reshape(tok_rows, 2 * channels)], axis=1
    )
    placed = (
        jnp.zeros((3, 3, channels), jnp.float32)
        .at[:, 0, :]
        .set(tap_terms(grad_query, src_seq, before, keep_one, keep_two))
    )
    placed = lax.dynamic_update_slice(placed, kv_taps, (0, 1, shard_index * per_shard))
    tap_sum = placed.reshape(3, 3 * channels)
    grad_taps = lax.psum(tap_sum, ("dp", "ctx")) * grad_scale
    resid_sum, skip_sum = lax.psum((grad_resid, skip_part), "dp")
    return (grad_feats[None], grad_taps, resid_sum * grad_scale, skip_sum * grad_scale)


def solution(mesh):
    return jax.shard_map(
        per_device,
        mesh=mesh,
        in_specs=(
            P("dp", "ctx", None),
            P("dp", "ctx", None),
            P("dp", None),
            P(),
            P(None, "ctx"),
            P(None, "ctx"),
            P("ctx"),
        ),
        out_specs=(P("dp", "ctx", None), P(), P(None, "ctx"), P("ctx")),
        check_vma=False,
    )
```

profile of v0, /device:TPU:1, one launch (start us, length us, event | category | flops | bytes accessed | tf_op | source)
XLA Modules:
  0.0 609.8 jit_solution(1691059669882293001)
XLA Ops:
  10.4 5.2 collective-permute-start.1
  17.9 7.7 %collective-permute-done.1 = bf16[2,2048]{0,1:T(8,128)(2,1)} collective-permute-done((bf16[2,2048]{0,1:T(8,128)(2,1)}, bf16[2,2048]{0,1:T(8,128)(2,1)}, u32[]{:S(2)}, u32[]{:S(2)}) %collective-permute-start.1) | collective-permute-done | bytes 8224 | tf_op jit(solution)/shard_map/ppermute | solution.py:13
  28.8 8.9 %copy.348 = bf16[128,1,2048]{0,1,2:T(2,128)(2,1)} copy(bf16[128,1,2048]{0,2,1:T(8,128)(2,1)S(1)} %fusion.46) | data formatting | bytes 1048576 | tf_op jit(solution)/shard_map/broadcast_in_dim | solution.py:164
  38.2 12.5 %reduce.26 = bf16[2048,128]{1,0:T(8,128)(2,1)S(1)} reduce(bf16[2048,1,128]{2,1,0:T(2,128)(2,1)} %bitcast.298, bf16[]{:T(256)} %broadcast.332), dimensions={1}, to_apply=%bitcast.221.reduce_sub_computation | reduce | bytes 1048578
  51.7 13.2 %all-to-all-start.2 = ((bf16[32,2,4096]{2,1,0:T(2,128)(2,1)}), bf16[32,2,4096]{2,1,0:T(2,128)(2,1)S(1)}, u32[]{:S(2)}, u32[]{:S(2)}) async-start(bf16[32,2,4096]{2,1,0:T(2,128)(2,1)} %reshape.467), calls=%async_computation.2 | async-start | bytes 1048576 | tf_op jit(solution)/shard_map/all_to_all | solution.py:166
  65.0 9.5 %copy.215 = bf16[128,2,2048]{0,1,2:T(2,128)(2,1)} copy(bf16[128,2,2048]{0,2,1:T(8,128)(2,1)S(1)} %bitcast.297) | data formatting | bytes 2097152 | tf_op jit(solution)/shard_map/reshape | solution.py:163
  77.7 8.6 %all-to-all-start = ((bf16[128,2,2048]{0,1,2:T(2,128)(2,1)}), bf16[128,2,2048]{0,1,2:T(2,128)(2,1)S(1)}, u32[]{:S(2)}, u32[]{:S(2)}) async-start(bf16[128,2,2048]{0,1,2:T(2,128)(2,1)} %copy.215), calls=%async_computation | async-start | bytes 2097152 | tf_op jit(solution)/shard_map/all_to_all | solution.py:165
  92.9 13.4 %rev.13 = f32[4096,64]{0,1:T(8,128)S(1)} reverse(f32[4096,64]{0,1:T(8,128)} %bitcast.302), dimensions={0} | reverse | bytes 2097152 | tf_op jit(solution)/shard_map/rev | solution.py:180
  112.3 3.6 multiply_reduce_fusion.2
  122.3 90.9 %while.32 = (s32[]{:T(128)}, f32[8,4,128,64]{2,1,0,3:T(4,128)S(1)}, f32[8,4,16,64]{3,2,1,0:T(8,128)S(1)}, f32[8,16,64]{2,1,0:T(8,128)}, f32[8,4,16,64]{3,2,1,0:T...) while((s32[]{:T(128)}, f32[8,4,128,64]{2,1,0,3:T(4,128)S(1)}, ...), condition=%wide.region_12.13_spmd.clone, body=%wide.region_11.12_spmd.clone.sunk | while | flops 820528128 | bytes 18125500 | solution.py:109
  129.3 3.5 fusion.87
  140.6 3.5 fusion.87
  152.0 3.5 fusion.87
  163.3 3.5 fusion.87
  174.6 3.5 fusion.87
  186.0 3.5 fusion.87
  215.4 52.8 %while.31 = (s32[]{:T(128)}, f32[8,4,128,64]{2,1,0,3:T(4,128)}, f32[8,4,16,64]{3,2,1,0:T(8,128)}, s32[8,4,128]{2,1,0:T(4,128)S(1)}, f32[8,4,128,64]{2,1,0,3:T(4,...) while((s32[]{:T(128)}, f32[8,4,128,64]{2,1,0,3:T(4,128)}, ...), condition=%wide.region_5.6_spmd.clone, body=%wide.region_4.5_spmd.clone.sunk | while | flops 807780352 | bytes 14388493 | solution.py:109
  294.5 8.6 %all-to-all-start.1 = ((bf16[32,2,4096]{2,1,0:T(2,128)(2,1)}), bf16[32,2,4096]{2,1,0:T(2,128)(2,1)}, u32[]{:S(2)}, u32[]{:S(2)}) async-start(bf16[32,2,4096]{2,1,0:T(2,128)(2,1)} %reshape.471), calls=%async_computation.1 | async-start | bytes 1048576 | tf_op jit(solution)/shard_map/all_to_all | solution.py:198
  309.8 14.4 %all-reduce.23 = (f32[16,64]{1,0:T(8,128)S(1)}, f32[64]{0:T(128)S(1)}) all-reduce(f32[16,64]{1,0:T(8,128)S(1)} %add.336, f32[64]{0:T(128)S(1)} %copy-done.70), channel_id=1, replica_groups=mesh['dp'=8,'ctx'=32] {'dp'}, use_global_device_ids=true, to_apply=%region_26.27 | all-reduce | flops 1088 | bytes 8704 | tf_op jit(solution)/shard_map/psum | solution.py:216
  325.3 9.2 %all-to-all-start.3 = ((bf16[32,2,8192]{2,1,0:T(2,128)(2,1)}), bf16[32,2,8192]{2,1,0:T(2,128)(2,1)S(1)}, u32[]{:S(2)}, u32[]{:S(2)}) async-start(bf16[32,2,8192]{2,1,0:T(2,128)(2,1)} %reshape.469), calls=%async_computation.3 | async-start | bytes 2097152 | tf_op jit(solution)/shard_map/all_to_all | solution.py:199
  334.6 4.1 reshape.472
  338.8 3.6 copy.226
  351.0 6.3 %collective-permute-done = f32[2,2048]{1,0:T(2,128)S(1)} collective-permute-done((f32[2,2048]{1,0:T(2,128)S(1)}, f32[2,2048]{1,0:T(2,128)S(1)}, u32[]{:S(2)}, u32[]{:S(2)}) %collective-permute-start) | collective-permute-done | bytes 16416 | tf_op jit(solution)/shard_map/ppermute | solution.py:13
  360.5 233.8 %all-reduce.26.cloned.1.call-done = f32[3,6144]{1,0:T(4,128)} async-done(((f32[3,6144]{1,0:T(4,128)}), f32[3,6144]{1,0:T(4,128)}) %all-reduce.26.cloned.1.call-update) | async-done | bytes 73744 | tf_op jit(solution)/shard_map/psum | solution.py:215
  (665 shorter events, 208.3 us)
Async XLA Ops:
  9.1 55.8 %copy-start.2 = (bf16[1,128,6144]{1,2,0:T(8,128)(2,1)}, bf16[1,128,6144]{1,2,0:T(8,128)(2,1)S(1)}, u32[]{:S(2)}) copy-start(bf16[1,128,6144]{1,2,0:T(8,128)(2,1)S(1)} %copy.214) | copy-start | bytes 4718596
  10.4 15.3 %collective-permute-start.1 = (bf16[2,2048]{0,1:T(8,128)(2,1)}, bf16[2,2048]{0,1:T(8,128)(2,1)}, u32[]{:S(2)}, u32[]{:S(2)}) collective-permute-start(bf16[2,2048]{0,1:T(8,128)(2,1)} %slice.487), channel_id=1, source_target_pairs={{0,1},{1,2},{2,3},{3,4},{4,5},{5,6},{6,7},{7,8},{8,9},{9,10},{10,1... | collective-permute-start | bytes 24584 | tf_op jit(solution)/shard_map/ppermute | solution.py:13
  15.6 13.1 %copy-start.9 = (f32[128,2048]{0,1:T(8,128)}, f32[128,2048]{0,1:T(8,128)S(1)}, u32[]{:S(2)}) copy-start(f32[128,2048]{0,1:T(8,128)S(1)} %slice_convert_fusion) | copy-start | bytes 3145732
  15.9 12.8 %copy-start.38 = (f32[1,2048]{1,0:T(1,128)}, f32[1,2048]{1,0:T(1,128)S(1)}, u32[]{:S(2)}) copy-start(f32[1,2048]{1,0:T(1,128)S(1)} %get-tuple-element.452) | copy-start | bytes 24580
  15.9 12.8 %copy-start.40 = (f32[1,2048]{1,0:T(1,128)}, f32[1,2048]{1,0:T(1,128)S(1)}, u32[]{:S(2)}) copy-start(f32[1,2048]{1,0:T(1,128)S(1)} %get-tuple-element.453) | copy-start | bytes 24580
  15.9 12.8 %copy-start.42 = (f32[1,2048]{1,0:T(1,128)}, f32[1,2048]{1,0:T(1,128)S(1)}, u32[]{:S(2)}) copy-start(f32[1,2048]{1,0:T(1,128)S(1)} %get-tuple-element.454) | copy-start | bytes 24580
  16.6 12.1 %copy-start.50 = (f32[128]{0:T(128)}, f32[128]{0:T(128)S(1)}, u32[]{:S(2)}) copy-start(f32[128]{0:T(128)S(1)} %get-tuple-element.477) | copy-start | bytes 1540
  16.6 12.1 %copy-start.52 = (f32[128]{0:T(128)}, f32[128]{0:T(128)S(1)}, u32[]{:S(2)}) copy-start(f32[128]{0:T(128)S(1)} %get-tuple-element.478) | copy-start | bytes 1540
  51.7 26.0 %all-to-all-start.2 = ((bf16[32,2,4096]{2,1,0:T(2,128)(2,1)}), bf16[32,2,4096]{2,1,0:T(2,128)(2,1)S(1)}, u32[]{:S(2)}, u32[]{:S(2)}) async-start(bf16[32,2,4096]{2,1,0:T(2,128)(2,1)} %reshape.467), calls=%async_computation.2 | async-start | bytes 1048576 | tf_op jit(solution)/shard_map/all_to_all | solution.py:166
  77.7 33.2 %all-to-all-start = ((bf16[128,2,2048]{0,1,2:T(2,128)(2,1)}), bf16[128,2,2048]{0,1,2:T(2,128)(2,1)S(1)}, u32[]{:S(2)}, u32[]{:S(2)}) async-start(bf16[128,2,2048]{0,1,2:T(2,128)(2,1)} %copy.215), calls=%async_computation | async-start | bytes 2097152 | tf_op jit(solution)/shard_map/all_to_all | solution.py:165
  86.4 25.9 %copy-start.54 = (f32[64]{0:T(128)}, f32[64]{0:T(128)S(1)}, u32[]{:S(2)}) copy-start(f32[64]{0:T(128)S(1)} %get-tuple-element.446) | copy-start | bytes 772
  86.4 25.9 %copy-start.56 = (f32[64]{0:T(128)}, f32[64]{0:T(128)S(1)}, u32[]{:S(2)}) copy-start(f32[64]{0:T(128)S(1)} %get-tuple-element.447) | copy-start | bytes 772
  86.4 25.9 %copy-start.58 = (f32[64]{0:T(128)}, f32[64]{0:T(128)S(1)}, u32[]{:S(2)}) copy-start(f32[64]{0:T(128)S(1)} %get-tuple-element.448) | copy-start | bytes 772
  86.4 25.9 %copy-start.60 = (f32[64]{0:T(128)}, f32[64]{0:T(128)S(1)}, u32[]{:S(2)}) copy-start(f32[64]{0:T(128)S(1)} %get-tuple-element.449) | copy-start | bytes 772
  86.4 25.8 %copy-start.62 = (f32[64]{0:T(128)}, f32[64]{0:T(128)S(1)}, u32[]{:S(2)}) copy-start(f32[64]{0:T(128)S(1)} %get-tuple-element.450) | copy-start | bytes 772
  86.4 25.8 %copy-start.64 = (f32[64]{0:T(128)}, f32[64]{0:T(128)S(1)}, u32[]{:S(2)}) copy-start(f32[64]{0:T(128)S(1)} %get-tuple-element.451) | copy-start | bytes 772
  89.0 23.3 %copy-start.34 = (f32[4096]{0:T(1024)}, f32[4096]{0:T(1024)S(1)}, u32[]{:S(2)}) copy-start(f32[4096]{0:T(1024)S(1)} %get-tuple-element.468) | copy-start | bytes 49156
  89.0 23.3 %copy-start.36 = (f32[4096]{0:T(1024)}, f32[4096]{0:T(1024)S(1)}, u32[]{:S(2)}) copy-start(f32[4096]{0:T(1024)S(1)} %get-tuple-element.469) | copy-start | bytes 49156
  291.4 11.7 %copy-start.61 = (f32[64]{0:T(128)S(1)}, f32[64]{0:T(128)}, u32[]{:S(2)}) copy-start(f32[64]{0:T(128)} %copy-done.60) | copy-start | bytes 772
  291.4 11.7 %copy-start.63 = (f32[64]{0:T(128)S(1)}, f32[64]{0:T(128)}, u32[]{:S(2)}) copy-start(f32[64]{0:T(128)} %copy-done.62) | copy-start | bytes 772
  294.5 30.8 %all-to-all-start.1 = ((bf16[32,2,4096]{2,1,0:T(2,128)(2,1)}), bf16[32,2,4096]{2,1,0:T(2,128)(2,1)}, u32[]{:S(2)}, u32[]{:S(2)}) async-start(bf16[32,2,4096]{2,1,0:T(2,128)(2,1)} %reshape.471), calls=%async_computation.1 | async-start | bytes 1048576 | tf_op jit(solution)/shard_map/all_to_all | solution.py:198
  325.3 270.5 %all-to-all-start.3 = ((bf16[32,2,8192]{2,1,0:T(2,128)(2,1)}), bf16[32,2,8192]{2,1,0:T(2,128)(2,1)S(1)}, u32[]{:S(2)}, u32[]{:S(2)}) async-start(bf16[32,2,8192]{2,1,0:T(2,128)(2,1)} %reshape.469), calls=%async_computation.3 | async-start | bytes 2097152 | tf_op jit(solution)/shard_map/all_to_all | solution.py:199
  334.6 259.7 %all-reduce.26.cloned.1.call-start = ((), (), s32[]{:S(2)}) async-start(), calls=%async_computation.4 | async-start | bytes 196608 | tf_op jit(solution)/shard_map/psum | solution.py:215
  348.5 8.8 %collective-permute-start = (f32[2,2048]{1,0:T(2,128)S(1)}, f32[2,2048]{1,0:T(2,128)S(1)}, u32[]{:S(2)}, u32[]{:S(2)}) collective-permute-start(f32[2,2048]{1,0:T(2,128)S(1)} %copy.228), channel_id=1, source_target_pairs={{1,0},{2,1},{3,2},{4,3},{5,4},{6,5},{7,6},{8,7},{9,8},{10,9},{11,1... | collective-permute-start | bytes 49160 | tf_op jit(solution)/shard_map/ppermute | solution.py:13
  (98 other events, 338.2 us)
Sparse Core Ops, SparseCore 0:
  351.1 243.1 all-reduce.25
where the time goes:
time: 621 us; the launch traced here: 610 us
  waiting for transfers between devices  252 us (41%)
  local copies, waits for them, and re-layouts  151 us (24%)
  other arithmetic  67.8 us (11%)
  matrix products  60.7 us (10%)
  starting transfers between devices  46 us (7%)
  between operations  15.7 us (3%)
  blocking collectives  14.4 us (2%)
    psum x1, waiting for transfers between devices, per_device(): grad_taps = lax.psum(tap_sum, ('dp', 'ctx')) * grad_scale  234 us
    dot_general x8, matrix products, group_fn(): jnp.einsum('pic,pimc->mc', other_blk, inner_state, precision=lax.Precisio...  27.9 us
    unnamed x151, local copies, waits for them, and re-layouts  23.1 us
    dynamic_slice x40, local copies, waits for them, and re-layouts, modal_sweep(): lax.map(group_fn, (src_groups, seg_groups, other_groups))  22.3 us
    dot_general x16, matrix products, group_fn(): jnp.einsum('pij,pjk->pik', joined_mask, lifted, precision=lax.Precision.H...  19.2 us
    slice x16, local copies, waits for them, and re-layouts, group_fn(): last_row = inner_state[:, -1]  18.7 us
    dynamic_update_slice x64, local copies, waits for them, and re-layouts, modal_sweep(): lax.map(group_fn, (src_groups, seg_groups, other_groups))  18.4 us
    psum x1, blocking collectives, per_device(): resid_sum, skip_sum = lax.psum((grad_resid, skip_part), 'dp')  14.4 us
  transfers between devices with their start and end apart: 7, of which 5 were waited for; matrix products, arithmetic and copies ran while one was open for 10% of the time, Pallas kernels for 0%

commit v1 on v0

--- a/solution.py
+++ b/solution.py
@@ -212,7 +212,7 @@
     )
     placed = lax.dynamic_update_slice(placed, kv_taps, (0, 1, shard_index * per_shard))
     tap_sum = placed.reshape(3, 3 * channels)
-    grad_taps = lax.psum(tap_sum, ("dp", "ctx")) * grad_scale
+    grad_taps = lax.psum(lax.psum(tap_sum, "ctx"), "dp") * grad_scale
     resid_sum, skip_sum = lax.psum((grad_resid, skip_part), "dp")
     return (grad_feats[None], grad_taps, resid_sum * grad_scale, skip_sum * grad_scale)
 

time: 621 us -> 583 us (0.939)
  the two profiles are of different devices: /device:TPU:1 before, /device:TPU:8 now
where the time goes in v1:
time: 583 us; the launch traced here: 572 us
  waiting for transfers between devices  213 us (37%)
  local copies, waits for them, and re-layouts  153 us (26%)
  other arithmetic  70.9 us (12%)
  matrix products  60.7 us (10%)
  starting transfers between devices  42.8 us (7%)
  between operations  15.7 us (3%)
  blocking collectives  14 us (2%)
    psum x2, waiting for transfers between devices, per_device(): grad_taps = lax.psum(lax.psum(tap_sum, 'ctx'), 'dp') * grad_scale  190 us
    dot_general x8, matrix products, group_fn(): jnp.einsum('pic,pimc->mc', other_blk, inner_state, precision=lax.Precisio...  27.9 us
    unnamed x145, local copies, waits for them, and re-layouts  25.1 us
    dynamic_slice x40, local copies, waits for them, and re-layouts, modal_sweep(): lax.map(group_fn, (src_groups, seg_groups, other_groups))  22.3 us
    dot_general x16, matrix products, group_fn(): jnp.einsum('pij,pjk->pik', joined_mask, lifted, precision=lax.Precision.H...  19.2 us
    slice x16, local copies, waits for them, and re-layouts, group_fn(): last_row = inner_state[:, -1]  18.7 us
    dynamic_update_slice x64, local copies, waits for them, and re-layouts, modal_sweep(): lax.map(group_fn, (src_groups, seg_groups, other_groups))  18.4 us
    ppermute x2, waiting for transfers between devices, from_behind(): return lax.ppermute(block, axis, route)  16.3 us
  transfers between devices with their start and end apart: 8, of which 6 were waited for; matrix products, arithmetic and copies ran while one was open for 11% of the time, Pallas kernels for 0%

profile of v1, /device:TPU:8, one launch (start us, length us, event | category | flops | bytes accessed | tf_op | source)
XLA Modules:
  0.0 572.0 jit_solution(1992075215825499925)
XLA Ops:
  10.4 3.8 collective-permute-start.1
  16.6 13.6 %collective-permute-done.1 = bf16[2,2048]{0,1:T(8,128)(2,1)} collective-permute-done((bf16[2,2048]{0,1:T(8,128)(2,1)}, bf16[2,2048]{0,1:T(8,128)(2,1)}, u32[]{:S(2)}, u32[]{:S(2)}) %collective-permute-start.1) | collective-permute-done | bytes 8224 | tf_op jit(solution)/shard_map/ppermute | solution.py:13
  33.4 8.9 %copy.348 = bf16[128,1,2048]{0,1,2:T(2,128)(2,1)} copy(bf16[128,1,2048]{0,2,1:T(8,128)(2,1)S(1)} %fusion.46) | data formatting | bytes 1048576 | tf_op jit(solution)/shard_map/broadcast_in_dim | solution.py:164
  42.9 12.5 %reduce.26 = bf16[2048,128]{1,0:T(8,128)(2,1)S(1)} reduce(bf16[2048,1,128]{2,1,0:T(2,128)(2,1)} %bitcast.298, bf16[]{:T(256)} %broadcast.332), dimensions={1}, to_apply=%bitcast.221.reduce_sub_computation | reduce | bytes 1048578
  56.3 9.2 %all-to-all-start.2 = ((bf16[32,2,4096]{2,1,0:T(2,128)(2,1)}), bf16[32,2,4096]{2,1,0:T(2,128)(2,1)S(1)}, u32[]{:S(2)}, u32[]{:S(2)}) async-start(bf16[32,2,4096]{2,1,0:T(2,128)(2,1)} %reshape.467), calls=%async_computation.2 | async-start | bytes 1048576 | tf_op jit(solution)/shard_map/all_to_all | solution.py:166
  65.7 9.5 %copy.215 = bf16[128,2,2048]{0,1,2:T(2,128)(2,1)} copy(bf16[128,2,2048]{0,2,1:T(8,128)(2,1)S(1)} %bitcast.297) | data formatting | bytes 2097152 | tf_op jit(solution)/shard_map/reshape | solution.py:163
  80.0 7.0 %all-to-all-start = ((bf16[128,2,2048]{0,1,2:T(2,128)(2,1)}), bf16[128,2,2048]{0,1,2:T(2,128)(2,1)S(1)}, u32[]{:S(2)}, u32[]{:S(2)}) async-start(bf16[128,2,2048]{0,1,2:T(2,128)(2,1)} %copy.215), calls=%async_computation | async-start | bytes 2097152 | tf_op jit(solution)/shard_map/all_to_all | solution.py:165
  93.6 13.4 %rev.13 = f32[4096,64]{0,1:T(8,128)S(1)} reverse(f32[4096,64]{0,1:T(8,128)} %bitcast.302), dimensions={0} | reverse | bytes 2097152 | tf_op jit(solution)/shard_map/rev | solution.py:180
  108.7 3.5 all-to-all-done
  113.7 3.6 multiply_reduce_fusion.2
  123.7 90.9 %while.32 = (s32[]{:T(128)}, f32[8,4,128,64]{2,1,0,3:T(4,128)S(1)}, f32[8,4,16,64]{3,2,1,0:T(8,128)S(1)}, f32[8,16,64]{2,1,0:T(8,128)}, f32[8,4,16,64]{3,2,1,0:T...) while((s32[]{:T(128)}, f32[8,4,128,64]{2,1,0,3:T(4,128)S(1)}, ...), condition=%wide.region_12.13_spmd.clone, body=%wide.region_11.12_spmd.clone.sunk | while | flops 820528128 | bytes 18125500 | solution.py:109
  130.8 3.5 fusion.87
  142.1 3.5 fusion.87
  153.4 3.5 fusion.87
  164.8 3.5 fusion.87
  216.8 52.8 %while.31 = (s32[]{:T(128)}, f32[8,4,128,64]{2,1,0,3:T(4,128)}, f32[8,4,16,64]{3,2,1,0:T(8,128)}, s32[8,4,128]{2,1,0:T(4,128)S(1)}, f32[8,4,128,64]{2,1,0,3:T(4,...) while((s32[]{:T(128)}, f32[8,4,128,64]{2,1,0,3:T(4,128)}, ...), condition=%wide.region_5.6_spmd.clone, body=%wide.region_4.5_spmd.clone.sunk | while | flops 807780352 | bytes 14388493 | solution.py:109
  297.5 7.9 %all-to-all-start.1 = ((bf16[32,2,4096]{2,1,0:T(2,128)(2,1)}), bf16[32,2,4096]{2,1,0:T(2,128)(2,1)}, u32[]{:S(2)}, u32[]{:S(2)}) async-start(bf16[32,2,4096]{2,1,0:T(2,128)(2,1)} %reshape.471), calls=%async_computation.1 | async-start | bytes 1048576 | tf_op jit(solution)/shard_map/all_to_all | solution.py:198
  315.6 14.0 %all-reduce.23 = (f32[16,64]{1,0:T(8,128)S(1)}, f32[64]{0:T(128)S(1)}) all-reduce(f32[16,64]{1,0:T(8,128)S(1)} %add.338, f32[64]{0:T(128)S(1)} %copy-done.67), channel_id=1, replica_groups=mesh['dp'=8,'ctx'=32] {'dp'}, use_global_device_ids=true, to_apply=%region_27.28 | all-reduce | flops 1088 | bytes 8704 | tf_op jit(solution)/shard_map/psum | solution.py:216
  330.2 9.5 %all-to-all-start.3 = ((bf16[32,2,8192]{2,1,0:T(2,128)(2,1)}), bf16[32,2,8192]{2,1,0:T(2,128)(2,1)S(1)}, u32[]{:S(2)}, u32[]{:S(2)}) async-start(bf16[32,2,8192]{2,1,0:T(2,128)(2,1)} %reshape.469), calls=%async_computation.3 | async-start | bytes 2097152 | tf_op jit(solution)/shard_map/all_to_all | solution.py:199
  339.7 4.1 reshape.472
  343.9 3.6 copy.226
  354.8 5.4 collective-permute-start
  363.8 129.1 %all-reduce.27.cloned.1.call-done = f32[3,6144]{1,0:T(4,128)} async-done(((f32[3,6144]{1,0:T(4,128)}), f32[3,6144]{1,0:T(4,128)}) %all-reduce.27.cloned.1.call-update) | async-done | bytes 73744 | tf_op jit(solution)/shard_map/psum | solution.py:215
  495.7 60.8 %all-reduce.29.cloned.1.call-done = f32[3,6144]{1,0:T(4,128)} async-done(((f32[3,6144]{1,0:T(4,128)}), f32[3,6144]{1,0:T(4,128)}) %all-reduce.29.cloned.1.call-update) | async-done | bytes 73744 | tf_op jit(solution)/shard_map/psum | solution.py:215
  (662 shorter events, 220.4 us)
Async XLA Ops:
  9.1 56.5 %copy-start.2 = (bf16[1,128,6144]{1,2,0:T(8,128)(2,1)}, bf16[1,128,6144]{1,2,0:T(8,128)(2,1)S(1)}, u32[]{:S(2)}) copy-start(bf16[1,128,6144]{1,2,0:T(8,128)(2,1)S(1)} %copy.214) | copy-start | bytes 4718596
  10.4 19.9 %collective-permute-start.1 = (bf16[2,2048]{0,1:T(8,128)(2,1)}, bf16[2,2048]{0,1:T(8,128)(2,1)}, u32[]{:S(2)}, u32[]{:S(2)}) collective-permute-start(bf16[2,2048]{0,1:T(8,128)(2,1)} %slice.487), channel_id=1, source_target_pairs={{0,1},{1,2},{2,3},{3,4},{4,5},{5,6},{6,7},{7,8},{8,9},{9,10},{10,1... | collective-permute-start | bytes 24584 | tf_op jit(solution)/shard_map/ppermute | solution.py:13
  14.3 19.0 %copy-start.9 = (f32[128,2048]{0,1:T(8,128)}, f32[128,2048]{0,1:T(8,128)S(1)}, u32[]{:S(2)}) copy-start(f32[128,2048]{0,1:T(8,128)S(1)} %slice_convert_fusion) | copy-start | bytes 3145732
  14.5 18.8 %copy-start.35 = (f32[1,2048]{1,0:T(1,128)}, f32[1,2048]{1,0:T(1,128)S(1)}, u32[]{:S(2)}) copy-start(f32[1,2048]{1,0:T(1,128)S(1)} %get-tuple-element.452) | copy-start | bytes 24580
  56.3 23.7 %all-to-all-start.2 = ((bf16[32,2,4096]{2,1,0:T(2,128)(2,1)}), bf16[32,2,4096]{2,1,0:T(2,128)(2,1)S(1)}, u32[]{:S(2)}, u32[]{:S(2)}) async-start(bf16[32,2,4096]{2,1,0:T(2,128)(2,1)} %reshape.467), calls=%async_computation.2 | async-start | bytes 1048576 | tf_op jit(solution)/shard_map/all_to_all | solution.py:166
  80.0 32.2 %all-to-all-start = ((bf16[128,2,2048]{0,1,2:T(2,128)(2,1)}), bf16[128,2,2048]{0,1,2:T(2,128)(2,1)S(1)}, u32[]{:S(2)}, u32[]{:S(2)}) async-start(bf16[128,2,2048]{0,1,2:T(2,128)(2,1)} %copy.215), calls=%async_computation | async-start | bytes 2097152 | tf_op jit(solution)/shard_map/all_to_all | solution.py:165
  87.1 26.5 %copy-start.51 = (f32[64]{0:T(128)}, f32[64]{0:T(128)S(1)}, u32[]{:S(2)}) copy-start(f32[64]{0:T(128)S(1)} %get-tuple-element.446) | copy-start | bytes 772
  87.1 26.5 %copy-start.53 = (f32[64]{0:T(128)}, f32[64]{0:T(128)S(1)}, u32[]{:S(2)}) copy-start(f32[64]{0:T(128)S(1)} %get-tuple-element.447) | copy-start | bytes 772
  87.1 26.5 %copy-start.55 = (f32[64]{0:T(128)}, f32[64]{0:T(128)S(1)}, u32[]{:S(2)}) copy-start(f32[64]{0:T(128)S(1)} %get-tuple-element.448) | copy-start | bytes 772
  87.1 26.5 %copy-start.57 = (f32[64]{0:T(128)}, f32[64]{0:T(128)S(1)}, u32[]{:S(2)}) copy-start(f32[64]{0:T(128)S(1)} %get-tuple-element.449) | copy-start | bytes 772
  87.1 26.5 %copy-start.59 = (f32[64]{0:T(128)}, f32[64]{0:T(128)S(1)}, u32[]{:S(2)}) copy-start(f32[64]{0:T(128)S(1)} %get-tuple-element.450) | copy-start | bytes 772
  87.1 26.5 %copy-start.61 = (f32[64]{0:T(128)}, f32[64]{0:T(128)S(1)}, u32[]{:S(2)}) copy-start(f32[64]{0:T(128)S(1)} %get-tuple-element.451) | copy-start | bytes 772
  89.7 24.0 %copy-start.31 = (f32[4096]{0:T(1024)}, f32[4096]{0:T(1024)S(1)}, u32[]{:S(2)}) copy-start(f32[4096]{0:T(1024)S(1)} %get-tuple-element.468) | copy-start | bytes 49156
  89.7 24.0 %copy-start.33 = (f32[4096]{0:T(1024)}, f32[4096]{0:T(1024)S(1)}, u32[]{:S(2)}) copy-start(f32[4096]{0:T(1024)S(1)} %get-tuple-element.469) | copy-start | bytes 49156
  297.5 32.7 %all-to-all-start.1 = ((bf16[32,2,4096]{2,1,0:T(2,128)(2,1)}), bf16[32,2,4096]{2,1,0:T(2,128)(2,1)}, u32[]{:S(2)}, u32[]{:S(2)}) async-start(bf16[32,2,4096]{2,1,0:T(2,128)(2,1)} %reshape.471), calls=%async_computation.1 | async-start | bytes 1048576 | tf_op jit(solution)/shard_map/all_to_all | solution.py:198
  330.2 227.9 %all-to-all-start.3 = ((bf16[32,2,8192]{2,1,0:T(2,128)(2,1)}), bf16[32,2,8192]{2,1,0:T(2,128)(2,1)S(1)}, u32[]{:S(2)}, u32[]{:S(2)}) async-start(bf16[32,2,8192]{2,1,0:T(2,128)(2,1)} %reshape.469), calls=%async_computation.3 | async-start | bytes 2097152 | tf_op jit(solution)/shard_map/all_to_all | solution.py:199
  339.7 153.2 %all-reduce.27.cloned.1.call-start = ((), (), s32[]{:S(2)}) async-start(), calls=%async_computation.4 | async-start | bytes 196608 | tf_op jit(solution)/shard_map/psum | solution.py:215
  353.2 139.7 %copy-start.36 = (f32[1,2048]{1,0:T(1,128)S(1)}, f32[1,2048]{1,0:T(1,128)}, u32[]{:S(2)}) copy-start(f32[1,2048]{1,0:T(1,128)} %copy-done.35) | copy-start | bytes 24580
  353.2 139.7 %copy-start.38 = (f32[1,2048]{1,0:T(1,128)S(1)}, f32[1,2048]{1,0:T(1,128)}, u32[]{:S(2)}) copy-start(f32[1,2048]{1,0:T(1,128)} %copy-done.37) | copy-start | bytes 24580
  353.3 139.7 %copy-start.40 = (f32[1,2048]{1,0:T(1,128)S(1)}, f32[1,2048]{1,0:T(1,128)}, u32[]{:S(2)}) copy-start(f32[1,2048]{1,0:T(1,128)} %copy-done.39) | copy-start | bytes 24580
  353.3 139.7 %copy-start.65 = (f32[128]{0:T(128)S(1)}, f32[128]{0:T(128)}, u32[]{:S(2)}) copy-start(f32[128]{0:T(128)} %get-tuple-element.476) | copy-start | bytes 1540
  353.3 139.7 %copy-start.66 = (f32[128]{0:T(128)S(1)}, f32[128]{0:T(128)}, u32[]{:S(2)}) copy-start(f32[128]{0:T(128)} %get-tuple-element.479) | copy-start | bytes 1540
  354.5 202.1 %all-reduce.29.cloned.1.call-start = ((), (), s32[]{:S(2)}) async-start(), calls=%async_computation.5 | async-start | bytes 196608 | tf_op jit(solution)/shard_map/psum | solution.py:215
  354.8 8.5 %collective-permute-start = (f32[2,2048]{1,0:T(2,128)S(1)}, f32[2,2048]{1,0:T(2,128)S(1)}, u32[]{:S(2)}, u32[]{:S(2)}) collective-permute-start(f32[2,2048]{1,0:T(2,128)S(1)} %copy.228), channel_id=1, source_target_pairs={{1,0},{2,1},{3,2},{4,3},{5,4},{6,5},{7,6},{8,7},{9,8},{10,9},{11,1... | collective-permute-start | bytes 49160 | tf_op jit(solution)/shard_map/ppermute | solution.py:13
  (96 other events, 367.8 us)
Sparse Core Ops, SparseCore 0:
  354.6 138.2 all-reduce.26
  495.2 61.2 all-reduce.28
